TPU v7x, 32 devices: a whole 2x2x4 slice. The times are simulated.
32 devices in a mesh: grp: 2 (over y), seq: 4 (over z), ch: 2 (over x), sub: 2 (over core).
Axes of the slice: x: 2, y: 2, z: 4, core: 2. Of those that a mesh axis runs over, the one named last changes fastest.
Arguments:
- token_ids: int32 [2048], P(('grp', 'seq')), parts along dimension 0, may hold values from 0 to 511
- residual_in: bfloat16 [2048, 4096], P(('grp', 'seq'), ('ch', 'sub')), parts along dimension 0, may hold values from -6 to 6
- embedding: bfloat16 [512, 4096], P(None, ('ch', 'sub')), may hold values from -6 to 6
- in_weight: bfloat16 [4096, 3, 2048], P('seq', None, ('ch', 'sub')), may hold values from -0.09375 to 0.09375
- short_filter: float32 [3, 3, 2048], P(None, None, ('ch', 'sub')), may hold values from -3 to 3
- decay_rate: float32 [16, 2048], P(None, ('ch', 'sub')), may hold values from 1e-05 to 0.05
- residue: float32 [16, 2048], P(None, ('ch', 'sub')), may hold values from -0.24 to 0.24
- skip: float32 [2048], P(('ch', 'sub')), may hold values from -4 to 4
Outputs:
- mixed_out: bfloat16 [2048, 2048], P(('grp', 'seq'), ('ch', 'sub')), parts along dimension 0
There are 2 independent parts, one for each index of `grp`. A program takes and returns all parts, laid end to end along the dimension named above; an argument that names none is the same for every part. Nothing has to cross between parts.
All inputs are finite; a program needn't handle non-finite values.
Results may differ from a plain program's by a relative error of at most 0.0095.
Values may be sent and summed in bfloat16 or wider, within the bound.
A program may use at most 64 MiB of HBM per device.

v0:
```python
import jax
import jax.numpy as jnp
from jax import lax
from jax.sharding import PartitionSpec as P

PRECISE = lax.Precision.HIGHEST
TWO_PI = 6.283185307179586


def shifted(x, axis, by):
    peers = lax.axis_size(axis)
    pairs = [(i, i + by) for i in range(peers) if 0 <= i + by < peers]
    return lax.ppermute(x, axis, pairs)


def swapped(value, axis, apart):
    mask = 2**apart
    pairs = [(source, source ^ mask) for source in range(lax.axis_size(axis))]
    return lax.ppermute(value, axis, pairs)


def reversed_bits(number, bit_count):
    result = jnp.zeros_like(number)
    for section_bit in range(bit_count):
        result = result + (number >> section_bit & 1) * (1 << bit_count - 1 - section_bit)
    return result


def angle_table(left_idx, right_idx, period):
    wrapped = left_idx[:, None] * right_idx[None, :] % period
    return TWO_PI * wrapped.astype(jnp.float32) / period


def complex_mix(mat_re, mat_im, data_re, data_im):
    real_part = jnp.einsum("kr,rjc->kjc", mat_re, data_re, precision=PRECISE) - jnp.einsum(
        "kr,rjc->kjc", mat_im, data_im, precision=PRECISE
    )
    imag_part = jnp.einsum("kr,rjc->kjc", mat_re, data_im, precision=PRECISE) + jnp.einsum(
        "kr,rjc->kjc", mat_im, data_re, precision=PRECISE
    )
    return (real_part, imag_part)


def complex_dot(mat_re, mat_im, data_re, data_im):
    real_part = jnp.dot(mat_re, data_re, precision=PRECISE) - jnp.dot(
        mat_im, data_im, precision=PRECISE
    )
    imag_part = jnp.dot(mat_re, data_im, precision=PRECISE) + jnp.dot(
        mat_im, data_re, precision=PRECISE
    )
    return (real_part, imag_part)


def shards(token_ids, residual_in, embedding, in_weight, short_filter, decay_rate, residue, skip):
    tok_rows = residual_in.shape[0]
    vocab_size = embedding.shape[0]
    channels = skip.shape[0]
    seq_parts = lax.axis_size("seq")
    bit_count = seq_parts.bit_length() - 1
    my_index = lax.axis_index("seq")
    length = tok_rows * seq_parts
    padded_len = 2 * length
    group_rows = tok_rows // seq_parts
    onehot = (token_ids[:, None] == jnp.arange(vocab_size, dtype=jnp.int32)[None, :]).astype(
        jnp.bfloat16
    )
    embedded = jnp.dot(onehot, embedding, preferred_element_type=jnp.float32)
    inputs = (residual_in.astype(jnp.float32) + embedded).astype(jnp.bfloat16)
    features = lax.all_gather(inputs, ("ch", "sub"), axis=1, tiled=True)
    piece_rows = lax.all_gather(in_weight, "seq", axis=0, tiled=True)
    flat_piece = piece_rows.reshape(piece_rows.shape[0], 3 * channels)
    projected = jnp.dot(features, flat_piece, preferred_element_type=jnp.float32)
    projected = projected.astype(jnp.bfloat16).reshape(tok_rows, 3, channels)
    rim_rows = shifted(projected[tok_rows - 2 :], "seq", 1)
    extended = jnp.concatenate([rim_rows, projected], axis=0).astype(jnp.float32)
    mixed_in = (
        short_filter[0] * extended[2:]
        + short_filter[1] * extended[1:-1]
        + short_filter[2] * extended[:-2]
    )
    query_gate = mixed_in[:, 0]
    product = (mixed_in[:, 1] * mixed_in[:, 2]).astype(jnp.bfloat16)
    local_pos = jnp.arange(tok_rows, dtype=jnp.int32)
    sources = jnp.arange(seq_parts, dtype=jnp.int32)
    within_rows = my_index * group_rows + jnp.arange(group_rows, dtype=jnp.int32)
    block_pos = sources[:, None] * tok_rows + within_rows[None, :]
    block_angle = TWO_PI * block_pos.astype(jnp.float32) / padded_len
    pos_angle = TWO_PI * (my_index * tok_rows + local_pos).astype(jnp.float32) / padded_len
    values = product.astype(jnp.float32)
    state_re = jnp.concatenate([values, values * jnp.cos(pos_angle)[:, None]], -1)
    state_im = jnp.concatenate([jnp.zeros_like(values), -values * jnp.sin(pos_angle)[:, None]], -1)
    state_now = jnp.stack([state_re, state_im])
    for section_bit in range(bit_count - 1, -1, -1):
        half_span = 1 << section_bit
        partner = swapped(state_now.astype(jnp.bfloat16), "seq", section_bit).astype(
            state_now.dtype
        )
        upper_half = my_index >> section_bit & 1 == 1
        phase_now = TWO_PI * (my_index % half_span).astype(jnp.float32) / (2 * half_span)
        difference = partner - state_now
        rot_re = difference[0] * jnp.cos(phase_now) + difference[1] * jnp.sin(phase_now)
        rot_im = difference[1] * jnp.cos(phase_now) - difference[0] * jnp.sin(phase_now)
        state_now = jnp.where(upper_half, jnp.stack([rot_re, rot_im]), state_now + partner)
    own_freq = reversed_bits(my_index, bit_count)
    holders = reversed_bits(sources, bit_count)
    twist_angle = TWO_PI * (local_pos * own_freq % length).astype(jnp.float32) / length
    twist_re = jnp.cos(twist_angle)[:, None]
    twist_im = -jnp.sin(twist_angle)[:, None]
    spec_re = state_now[0] * twist_re - state_now[1] * twist_im
    spec_im = state_now[0] * twist_im + state_now[1] * twist_re
    kernel_table = angle_table(local_pos, local_pos, tok_rows)
    dft_re = jnp.cos(kernel_table)
    dft_im = -jnp.sin(kernel_table)
    spec_re, spec_im = complex_dot(dft_re, dft_im, spec_re, spec_im)
    parity = (jnp.arange(2 * channels, dtype=jnp.int32) >= channels).astype(jnp.int32)
    full_freq = 2 * (own_freq + seq_parts * local_pos)[:, None] + parity[None, :]
    freq_angle = TWO_PI * full_freq.astype(jnp.float32) / padded_len
    half_sine = jnp.sin(0.5 * freq_angle)
    sine_full = jnp.sin(freq_angle)
    sign_flip = 1.0 - 2.0 * parity.astype(jnp.float32)
    rates_both = jnp.concatenate([decay_rate, decay_rate], -1)
    residues_both = jnp.concatenate([residue, residue], -1)
    filt_re = jnp.zeros_like(spec_re)
    filt_im = jnp.zeros_like(spec_re)
    for mode_index in range(rates_both.shape[0]):
        rate_now = rates_both[mode_index]
        decay_now = jnp.exp(-rate_now)
        numerator = residues_both[mode_index] * (1.0 - sign_flip * jnp.exp(-rate_now * length))
        denom_re = -jnp.expm1(-rate_now) + 2.0 * decay_now * half_sine * half_sine
        denom_im = decay_now * sine_full
        scaled = numerator / (denom_re * denom_re + denom_im * denom_im)
        filt_re = filt_re + scaled * denom_re
        filt_im = filt_im - scaled * denom_im
    prod_re = spec_re * filt_re - spec_im * filt_im
    prod_im = spec_re * filt_im + spec_im * filt_re
    inv_re, inv_im = complex_dot(dft_re, -dft_im, prod_re, prod_im)
    back_re = inv_re * twist_re + inv_im * twist_im
    back_im = inv_im * twist_re - inv_re * twist_im
    returned = lax.all_to_all(
        jnp.stack([back_re, back_im]).reshape(2, 1, tok_rows, 2 * channels).astype(jnp.bfloat16),
        "seq",
        split_axis=2,
        concat_axis=1,
        tiled=True,
    ).astype(jnp.float32)
    inverse_angle = angle_table(sources, holders, seq_parts)
    block_re, block_im = complex_mix(
        jnp.cos(inverse_angle), jnp.sin(inverse_angle), returned[0], returned[1]
    )
    conv_blocks = (
        block_re[..., :channels]
        + jnp.cos(block_angle)[:, :, None] * block_re[..., channels:]
        - jnp.sin(block_angle)[:, :, None] * block_im[..., channels:]
    )
    conv_blocks = conv_blocks / padded_len
    conv_rows = lax.all_to_all(conv_blocks, "seq", split_axis=0, concat_axis=1, tiled=True)[0]
    mixed_out = (query_gate * (conv_rows + skip * product.astype(jnp.float32))).astype(jnp.bfloat16)
    return mixed_out


def solution(mesh):
    return jax.shard_map(
        shards,
        mesh=mesh,
        in_specs=(
            P(("grp", "seq")),
            P(("grp", "seq"), ("ch", "sub")),
            P(None, ("ch", "sub")),
            P("seq", None, ("ch", "sub")),
            P(None, None, ("ch", "sub")),
            P(None, ("ch", "sub")),
            P(None, ("ch", "sub")),
            P(("ch", "sub")),
        ),
        out_specs=P(("grp", "seq"), ("ch", "sub")),
        check_vma=False,
    )
```

profile of v0, /device:TPU:0, one launch (start us, length us, event | category | flops | bytes accessed | tf_op | source)
XLA Modules:
  0.0 444.1 jit_solution(15915545846270894361)
XLA Ops:
  6.5 1.2 copy-done
  7.8 2.3 fusion.5
  10.2 4.7 %copy.55 = bf16[1024,3,512]{0,2,1:T(8,128)(2,1)} copy(bf16[1024,3,512]{2,0,1:T(8,128)(2,1)} %param.11) | data formatting | bytes 6291456 | tf_op args[3]
  14.9 0.7 copy-done.6
  15.6 20.0 %all-gather.3.cloned.1.call-done = bf16[256,4096]{1,0:T(8,128)(2,1)} async-done(((bf16[256,1024]{1,0:T(8,128)(2,1)}), bf16[256,4096]{1,0:T(8,128)(2,1)}) %all-gather.3.cloned.1.call-update) | async-done | bytes 2097168 | tf_op jit(solution)/shard_map/all_gather | solution.py:69
  35.6 219.8 %all-gather.5.cloned.1.call-done = bf16[4096,3,512]{0,2,1:T(8,128)(2,1)} async-done(((bf16[1024,3,512]{0,2,1:T(8,128)(2,1)}), bf16[4096,3,512]{0,2,1:T(8,128)(2,1)}) %all-gather.5.cloned.1.call-update) | async-done | bytes 12582928 | tf_op jit(solution)/shard_map/all_gather | solution.py:70
  255.4 8.7 %convolution_convert_fusion = bf16[256,1536]{1,0:T(8,128)(2,1)S(1)} fusion(bf16[256,4096]{1,0:T(8,128)(2,1)} %all-gather.3.cloned.1.call-done, bf16[4096,1536]{0,1:T(8,128)(2,1)} %bitcast.208), kind=kOutput, calls=%fused_computation.4 | convolution fusion | flops 3221618688 | bytes 15466496 | tf_op jit(solution)/shard_map/dot_general | solution.py:72
  264.0 1.5 collective-permute-start
  265.6 0.3 copy.57
  265.8 0.3 copy.58
  266.1 0.5 collective-permute-done
  266.7 0.2 maximum_convert_fusion
  266.9 0.5 fusion.2
  267.7 0.8 copy-done.3
  268.7 1.3 fusion.4
  269.9 3.5 collective-permute-start.1
  273.7 0.8 constant_dynamic-update-slice_fusion.3
  274.4 0.8 constant_dynamic-update-slice_fusion
  275.2 0.6 fusion.155
  275.8 42.2 %collective-permute-done.1 = bf16[2,256,1024]{2,1,0:T(8,128)(2,1)S(1)} collective-permute-done((bf16[2,256,1024]{2,1,0:T(8,128)(2,1)}, bf16[2,256,1024]{2,1,0:T(8,128)(2,1)S(1)}, u32[]{:S(2)}, u32[]{:S(2)}) %collective-permute-start.1) | collective-permute-done | bytes 1048608 | tf_op jit(solution)/shard_map/ppermute | solution.py:19
  318.0 0.3 convert_subtract_fusion.1
  318.4 0.6 copy-done.4
  319.0 0.3 multiply_add_fusion.4
  319.3 3.2 fusion.171
  322.5 0.6 add_multiply_fusion
  323.5 22.9 %collective-permute-done.2 = bf16[2,256,1024]{2,1,0:T(8,128)(2,1)S(1)} collective-permute-done((bf16[2,256,1024]{2,1,0:T(8,128)(2,1)}, bf16[2,256,1024]{2,1,0:T(8,128)(2,1)S(1)}, u32[]{:S(2)}, u32[]{:S(2)}) %collective-permute-start.2) | collective-permute-done | bytes 1048608 | tf_op jit(solution)/shard_map/ppermute | solution.py:19
  346.4 0.3 convert_subtract_fusion
  346.9 0.6 fusion.1
  347.5 2.2 fusion.72
  349.7 2.2 fusion.70
  352.0 2.2 convolution_subtract_fusion.2
  354.3 18.1 %multiply_add_fusion = (f32[256,1024]{1,0:T(8,128)S(1)}, f32[256,1024]{1,0:T(8,128)S(1)}, f32[256,1024]{1,0:T(8,128)S(1)}, f32[256,1024]{1,0:T(8,128)S(1)}) fusion(f32[256,1024]{1,0:T(8,128)S(1)} %convolution_subtract_fusion.2, f32[1024]{0:T(1024)S(1)} %bitcast.145, f32[1024]{0:T(1024)S(1)} %bitcast.146, f32[1024]{0:T(1024)S(1)} %bitcast.191, ...), kind=kOutput, calls=%fused_computation.59 | convolution fusion | flops 859242496 | bytes 8657920 | tf_op jit(solution)/shard_map/dot_general | solution.py:48
  372.3 2.0 fusion.66
  374.3 0.5 multiply_subtract_fusion
  374.8 2.0 fusion.68
  376.8 2.2 convolution_add_fusion.1
  379.0 2.3 fusion.38
  381.5 2.1 copy.59
  383.6 4.3 all-to-all-start
  388.2 23.8 %all-to-all-done = bf16[2,1,256,1024]{3,0,1,2:T(2,128)(2,1)S(1)} async-done(((bf16[2,1,256,1024]{3,0,1,2:T(2,128)(2,1)}), bf16[2,1,256,1024]{3,0,1,2:T(2,128)(2,1)S(1)}, u32[]{:S(2)}, u32[]{:S(2)}) %all-to-all-start) | async-done | bytes 1048608 | tf_op jit(solution)/shard_map/all_to_all | solution.py:139
  412.1 1.5 fusion.175
  413.7 1.1 fusion.52
  414.8 1.1 fusion.50
  416.0 1.1 fusion.47
  417.1 1.1 convolution_subtract_fusion
  418.2 0.3 fusion.42
  418.8 16.5 %all_to_all.8 = f32[4,64,512]{2,1,0:T(8,128)S(1)} all-to-all(f32[4,64,512]{2,1,0:T(8,128)S(1)} %copy.68), channel_id=1, replica_groups=mesh['grp'=2,'seq'=4,'ch'=2,'sub'=2] {'seq'}, dimensions={0} | all-to-all | bytes 1048576 | tf_op jit(solution)/shard_map/all_to_all | solution.py:156
  435.2 1.8 fusion.46
  (58 shorter events, 2.2 us)
Async XLA Ops:
  6.5 1.2 copy-start
  6.5 29.0 %all-gather.3.cloned.1.call-start = ((), (), s32[]{:S(2)}) async-start(), calls=%async_computation.2 | async-start | bytes 2621440 | tf_op jit(solution)/shard_map/all_gather | solution.py:69
  10.1 245.2 %all-gather.5.cloned.1.call-start = ((), (), s32[]{:S(2)}) async-start(), calls=%async_computation.3 | async-start | bytes 15728640 | tf_op jit(solution)/shard_map/all_gather | solution.py:70
  14.9 0.7 copy-start.6
  264.0 2.6 collective-permute-start
  267.4 1.2 copy-start.3
  268.6 49.7 %copy-start.2 = (f32[1,256,1024]{2,1,0:T(8,128)}, f32[1,256,1024]{2,1,0:T(8,128)S(1)}, u32[]{:S(2)}) copy-start(f32[1,256,1024]{2,1,0:T(8,128)S(1)} %maximum_bitcast_fusion) | copy-start | bytes 3145732
  268.6 5.0 %copy-start.5 = (f32[16,512]{1,0:T(8,128)S(1)}, f32[16,512]{1,0:T(8,128)}, u32[]{:S(2)}) copy-start(f32[16,512]{1,0:T(8,128)} %param.14) | copy-start | bytes 98308
  269.9 48.1 %collective-permute-start.1 = (bf16[2,256,1024]{2,1,0:T(8,128)(2,1)}, bf16[2,256,1024]{2,1,0:T(8,128)(2,1)S(1)}, u32[]{:S(2)}, u32[]{:S(2)}) collective-permute-start(bf16[2,256,1024]{2,1,0:T(8,128)(2,1)} %fusion.4), channel_id=1, source_target_pairs={{0,8},{4,12},{8,0},{12,4},{1,9},{5,13},{9,1},{13,5},{2,10},{6,14},... | collective-permute-start | bytes 3145736 | tf_op jit(solution)/shard_map/ppermute | solution.py:19
  318.0 1.0 copy-start.4
  322.5 23.9 %collective-permute-start.2 = (bf16[2,256,1024]{2,1,0:T(8,128)(2,1)}, bf16[2,256,1024]{2,1,0:T(8,128)(2,1)S(1)}, u32[]{:S(2)}, u32[]{:S(2)}) collective-permute-start(bf16[2,256,1024]{2,1,0:T(8,128)(2,1)} %get-tuple-element.8), channel_id=1, source_target_pairs={{0,4},{4,0},{8,12},{12,8},{1,5},{5,1},{9,13},{13,9},{2,6},{6,2},{1... | collective-permute-start | bytes 3145736 | tf_op jit(solution)/shard_map/ppermute | solution.py:19
  351.9 2.3 copy-start.7
  351.9 2.3 copy-start.8
  351.9 2.3 copy-start.9
  351.9 2.3 copy-start.10
  351.9 2.3 copy-start.11
  351.9 2.3 copy-start.12
  351.9 2.3 copy-start.13
  352.0 2.3 copy-start.15
  383.6 28.5 %all-to-all-start = ((bf16[2,1,256,1024]{3,0,1,2:T(2,128)(2,1)}), bf16[2,1,256,1024]{3,0,1,2:T(2,128)(2,1)S(1)}, u32[]{:S(2)}, u32[]{:S(2)}) async-start(bf16[2,1,256,1024]{3,0,1,2:T(2,128)(2,1)} %copy.59), calls=%async_computation | async-start | bytes 2097152 | tf_op jit(solution)/shard_map/all_to_all | solution.py:139
  418.2 17.0 %copy-start.14 = (f32[512]{0:T(512)S(1)}, f32[512]{0:T(512)}, u32[]{:S(2)}) copy-start(f32[512]{0:T(512)} %param.15) | copy-start | bytes 6148
  418.2 18.8 %copy-start.1 = (bf16[512,1024]{1,0:T(8,128)(2,1)S(1)}, bf16[512,1024]{1,0:T(8,128)(2,1)}, u32[]{:S(2)}) copy-start(bf16[512,1024]{1,0:T(8,128)(2,1)} %param.10) | copy-start | bytes 3145732
Sparse Core Ops, SparseCore 0:
  10.3 25.2 all-gather.2
  37.1 218.1 all-gather.4
where the time goes:
time: 448 us; the launch traced here: 444 us
  waiting for transfers between devices  329 us (73%)
  matrix products  48.5 us (11%)
  blocking collectives  16.5 us (4%)
  local copies, waits for them, and re-layouts  14.6 us (3%)
  between operations  14.2 us (3%)
  other arithmetic  11.7 us (3%)
  starting transfers between devices  9.35 us (2%)
    all_gather x1, waiting for transfers between devices, shards(): piece_rows = lax.all_gather(in_weight, 'seq', axis=0, tiled=True)  220 us
    ppermute x2, waiting for transfers between devices, swapped(): return lax.ppermute(value, axis, pairs)  65.1 us
    all_to_all x1, waiting for transfers between devices, shards(): lax.all_to_all(jnp.stack([back_re, back_im]).reshape(2, 1, tok_rows, 2 *...  23.8 us
    dot_general x2, matrix products, complex_dot(): jnp.dot(mat_im, data_re, precision=PRECISE)  20.3 us
    all_gather x1, waiting for transfers between devices, shards(): features = lax.all_gather(inputs, ('ch', 'sub'), axis=1, tiled=True)  20 us
    all_to_all x1, blocking collectives, shards(): lax.all_to_all(conv_blocks, 'seq', split_axis=0, concat_axis=1, tiled=True)  16.5 us
    unnamed x37, local copies, waits for them, and re-layouts  9.23 us
  transfers between devices with their start and end apart: 6, of which 6 were waited for; matrix products, arithmetic and copies ran while one was open for 2% of the time, Pallas kernels for 0%

commit v1 on v0

--- a/solution.py
+++ b/solution.py
@@ -5,6 +5,22 @@
 
 PRECISE = lax.Precision.HIGHEST
 TWO_PI = 6.283185307179586
+
+
+def pairwise_exchange(shard, axis, split, join):
+    ways, here = (lax.axis_size(axis), lax.axis_index(axis))
+    width = shard.shape[split] // ways
+    lengths = list(shard.shape)
+    lengths[split] = width
+    height = lengths[join]
+    lengths[join] = height * ways
+    full = jnp.zeros(lengths, shard.dtype)
+    for mask in range(ways):
+        part = lax.dynamic_slice_in_dim(shard, (here ^ mask) * width, width, axis=split)
+        if mask:
+            part = lax.ppermute(part, axis, [(d, d ^ mask) for d in range(ways)])
+        full = lax.dynamic_update_slice_in_dim(full, part, (here ^ mask) * height, axis=join)
+    return full
 
 
 def shifted(x, axis, by):
@@ -136,12 +152,11 @@
     inv_re, inv_im = complex_dot(dft_re, -dft_im, prod_re, prod_im)
     back_re = inv_re * twist_re + inv_im * twist_im
     back_im = inv_im * twist_re - inv_re * twist_im
-    returned = lax.all_to_all(
+    returned = pairwise_exchange(
         jnp.stack([back_re, back_im]).reshape(2, 1, tok_rows, 2 * channels).astype(jnp.bfloat16),
         "seq",
-        split_axis=2,
-        concat_axis=1,
-        tiled=True,
+        2,
+        1,
     ).astype(jnp.float32)
     inverse_angle = angle_table(sources, holders, seq_parts)
     block_re, block_im = complex_mix(

time: 448 us -> 444 us (level)
  waiting for transfers between devices: 329 us -> 313 us
  local copies, waits for them, and re-layouts: 14.6 us -> 27.7 us
    all_to_all x1 -> x0, waiting for transfers between devices: 23.8 us -> none  [shards(): lax.all_to_all(jnp.stack([back_re, back_im]).reshape(2, 1, tok_rows, 2 *...]
    dynamic_update_slice x0 -> x4, local copies, waits for them, and re-layouts: none -> 14.1 us  [pairwise_exchange(): lax.dynamic_update_slice_in_dim(full, part, (here ^ mask) * height, axis=...]
    ppermute x0 -> x3, waiting for transfers between devices: none -> 8.22 us  [pairwise_exchange(): part = lax.ppermute(part, axis, [(d, d ^ mask) for d in range(ways)])]
    unnamed x37 -> x39, local copies, waits for them, and re-layouts: 9.23 us -> 8.91 us
  transfers between devices with their start and end apart: 6 -> 8, of which waited for: 6 -> 7; matrix products, arithmetic and copies ran while one was open for 2% -> 5% of each run, Pallas kernels for 0% -> 0%
where the time goes in v1:
time: 444 us; the launch traced here: 440 us
  waiting for transfers between devices  313 us (70%)
  matrix products  48.7 us (11%)
  local copies, waits for them, and re-layouts  27.7 us (6%)
  blocking collectives  14.7 us (3%)
  between operations  14.3 us (3%)
  other arithmetic  12.7 us (3%)
  starting transfers between devices  9.46 us (2%)
    all_gather x1, waiting for transfers between devices, shards(): piece_rows = lax.all_gather(in_weight, 'seq', axis=0, tiled=True)  220 us
    ppermute x2, waiting for transfers between devices, swapped(): return lax.ppermute(value, axis, pairs)  64.1 us
    dot_general x2, matrix products, complex_dot(): jnp.dot(mat_im, data_re, precision=PRECISE)  20.5 us
    all_gather x1, waiting for transfers between devices, shards(): features = lax.all_gather(inputs, ('ch', 'sub'), axis=1, tiled=True)  20 us
    all_to_all x1, blocking collectives, shards(): lax.all_to_all(conv_blocks, 'seq', split_axis=0, concat_axis=1, tiled=True)  14.7 us
    dynamic_update_slice x4, local copies, waits for them, and re-layouts, pairwise_exchange(): lax.dynamic_update_slice_in_dim(full, part, (here ^ mask) * height, axis=...  14.1 us
    unnamed x39, local copies, waits for them, and re-layouts  8.91 us
  transfers between devices with their start and end apart: 8, of which 7 were waited for; matrix products, arithmetic and copies ran while one was open for 5% of the time, Pallas kernels for 0%

profile of v1, /device:TPU:0, one launch (start us, length us, event | category | flops | bytes accessed | tf_op | source)
XLA Modules:
  0.0 440.2 jit_solution(7021209127345861695)
XLA Ops:
  6.5 1.2 copy-done
  7.8 2.3 fusion.5
  10.2 4.7 %copy.34 = bf16[1024,3,512]{0,2,1:T(8,128)(2,1)} copy(bf16[1024,3,512]{2,0,1:T(8,128)(2,1)} %param.11) | data formatting | bytes 6291456 | tf_op args[3]
  14.9 0.7 copy-done.6
  15.6 20.0 %all-gather.3.cloned.1.call-done = bf16[256,4096]{1,0:T(8,128)(2,1)} async-done(((bf16[256,1024]{1,0:T(8,128)(2,1)}), bf16[256,4096]{1,0:T(8,128)(2,1)}) %all-gather.3.cloned.1.call-update) | async-done | bytes 2097168 | tf_op jit(solution)/shard_map/all_gather | solution.py:85
  35.6 219.8 %all-gather.5.cloned.1.call-done = bf16[4096,3,512]{0,2,1:T(8,128)(2,1)} async-done(((bf16[1024,3,512]{0,2,1:T(8,128)(2,1)}), bf16[4096,3,512]{0,2,1:T(8,128)(2,1)}) %all-gather.5.cloned.1.call-update) | async-done | bytes 12582928 | tf_op jit(solution)/shard_map/all_gather | solution.py:86
  255.4 8.7 %convolution_convert_fusion = bf16[256,1536]{1,0:T(8,128)(2,1)S(1)} fusion(bf16[256,4096]{1,0:T(8,128)(2,1)} %all-gather.3.cloned.1.call-done, bf16[4096,1536]{0,1:T(8,128)(2,1)} %bitcast.210), kind=kOutput, calls=%fused_computation.4 | convolution fusion | flops 3221618688 | bytes 15466496 | tf_op jit(solution)/shard_map/dot_general | solution.py:88
  264.0 1.5 collective-permute-start
  266.1 0.5 collective-permute-done
  266.9 0.5 fusion.2
  267.7 0.8 copy-done.3
  268.7 1.3 fusion.4
  269.9 3.5 collective-permute-start.1
  273.6 0.5 iota_multiply_fusion
  274.1 0.6 add_multiply_fusion
  274.8 0.8 constant_dynamic-update-slice_fusion.3
  275.5 0.8 constant_dynamic-update-slice_fusion
  276.3 0.6 fusion.151
  277.0 41.1 %collective-permute-done.1 = bf16[2,256,1024]{2,1,0:T(8,128)(2,1)S(1)} collective-permute-done((bf16[2,256,1024]{2,1,0:T(8,128)(2,1)}, bf16[2,256,1024]{2,1,0:T(8,128)(2,1)S(1)}, u32[]{:S(2)}, u32[]{:S(2)}) %collective-permute-start.1) | collective-permute-done | bytes 1048608 | tf_op jit(solution)/shard_map/ppermute | solution.py:35
  318.4 0.6 copy-done.4
  319.3 3.2 fusion.167
  322.5 0.5 iota_add_fusion
  323.4 23.0 %collective-permute-done.2 = bf16[2,256,1024]{2,1,0:T(8,128)(2,1)S(1)} collective-permute-done((bf16[2,256,1024]{2,1,0:T(8,128)(2,1)}, bf16[2,256,1024]{2,1,0:T(8,128)(2,1)S(1)}, u32[]{:S(2)}, u32[]{:S(2)}) %collective-permute-start.2) | collective-permute-done | bytes 1048608 | tf_op jit(solution)/shard_map/ppermute | solution.py:35
  346.9 0.6 fusion.1
  347.5 2.2 fusion.72
  349.7 2.2 fusion.70
  352.0 2.2 convolution_subtract_fusion.2
  354.3 18.3 %multiply_subtract_fusion = (f32[256,1024]{1,0:T(8,128)S(1)}, f32[256,1024]{1,0:T(8,128)S(1)}, f32[256,1024]{1,0:T(8,128)S(1)}, f32[256,1024]{1,0:T(8,128)S(1)}) fusion(f32[256,1024]{1,0:T(8,128)S(1)} %convolution_subtract_fusion.2, f32[1024]{0:T(1024)S(1)} %bitcast.147, f32[1024]{0:T(1024)S(1)} %bitcast.148, f32[1024]{0:T(1024)S(1)} %bitcast.193, ...), kind=kOutput, calls=%fused_computation.67 | convolution fusion | flops 859242496 | bytes 8657920 | tf_op jit(solution)/shard_map/dot_general | solution.py:64
  372.5 0.5 multiply_add_fusion
  373.0 2.0 fusion.66
  375.0 2.0 fusion.68
  377.0 2.3 convolution_add_fusion.1
  379.3 2.3 fusion.39
  382.2 3.3 collective-permute-start.4
  385.5 0.7 collective-permute-start.5
  387.3 3.5 dynamic_update_slice.12
  390.8 1.3 collective-permute-done.3
  392.1 1.4 copy.39
  393.5 3.5 dynamic_update_slice.13
  397.0 6.9 %collective-permute-done.4 = bf16[2,1,64,1024]{3,2,1,0:T(8,128)(2,1)S(1)} collective-permute-done((bf16[2,1,64,1024]{3,2,1,0:T(8,128)(2,1)S(1)}, bf16[2,1,64,1024]{3,2,1,0:T(8,128)(2,1)S(1)}, u32[]{:S(2)}, u32[]{:S(2)}) %collective-permute-start.4) | collective-permute-done | bytes 262176 | tf_op jit(solution)/shard_map/ppermute | solution.py:21
  404.3 3.5 dynamic_update_slice.14
  408.3 3.5 dynamic_update_slice.15
  411.8 1.0 fusion.49
  412.8 1.0 fusion.47
  413.9 1.0 fusion.48
  414.9 1.1 convolution_subtract_fusion
  416.6 14.7 %all_to_all.4 = f32[4,64,512]{2,1,0:T(8,128)S(1)} all-to-all(f32[4,64,512]{2,1,0:T(8,128)S(1)} %copy.44), channel_id=1, replica_groups=mesh['grp'=2,'seq'=4,'ch'=2,'sub'=2] {'seq'}, dimensions={0} | all-to-all | bytes 1048576 | tf_op jit(solution)/shard_map/all_to_all | solution.py:171
  431.3 1.8 fusion.46
  (71 shorter events, 5.9 us)
Async XLA Ops:
  6.5 1.2 copy-start
  6.5 29.0 %all-gather.3.cloned.1.call-start = ((), (), s32[]{:S(2)}) async-start(), calls=%async_computation.1 | async-start | bytes 2621440 | tf_op jit(solution)/shard_map/all_gather | solution.py:85
  10.1 245.2 %all-gather.5.cloned.1.call-start = ((), (), s32[]{:S(2)}) async-start(), calls=%async_computation.2 | async-start | bytes 15728640 | tf_op jit(solution)/shard_map/all_gather | solution.py:86
  14.9 0.7 copy-start.6
  264.0 2.6 collective-permute-start
  267.4 1.2 copy-start.3
  268.6 49.7 %copy-start.2 = (f32[1,256,1024]{2,1,0:T(8,128)}, f32[1,256,1024]{2,1,0:T(8,128)S(1)}, u32[]{:S(2)}) copy-start(f32[1,256,1024]{2,1,0:T(8,128)S(1)} %maximum_bitcast_fusion) | copy-start | bytes 3145732
  268.7 6.1 %copy-start.5 = (f32[16,512]{1,0:T(8,128)S(1)}, f32[16,512]{1,0:T(8,128)}, u32[]{:S(2)}) copy-start(f32[16,512]{1,0:T(8,128)} %param.14) | copy-start | bytes 98308
  269.9 48.1 %collective-permute-start.1 = (bf16[2,256,1024]{2,1,0:T(8,128)(2,1)}, bf16[2,256,1024]{2,1,0:T(8,128)(2,1)S(1)}, u32[]{:S(2)}, u32[]{:S(2)}) collective-permute-start(bf16[2,256,1024]{2,1,0:T(8,128)(2,1)} %fusion.4), channel_id=1, source_target_pairs={{0,8},{4,12},{8,0},{12,4},{1,9},{5,13},{9,1},{13,5},{2,10},{6,14},... | collective-permute-start | bytes 3145736 | tf_op jit(solution)/shard_map/ppermute | solution.py:35
  318.0 1.0 copy-start.4
  322.5 23.9 %collective-permute-start.2 = (bf16[2,256,1024]{2,1,0:T(8,128)(2,1)}, bf16[2,256,1024]{2,1,0:T(8,128)(2,1)S(1)}, u32[]{:S(2)}, u32[]{:S(2)}) collective-permute-start(bf16[2,256,1024]{2,1,0:T(8,128)(2,1)} %get-tuple-element.8), channel_id=1, source_target_pairs={{0,4},{4,0},{8,12},{12,8},{1,5},{5,1},{9,13},{13,9},{2,6},{6,2},{1... | collective-permute-start | bytes 3145736 | tf_op jit(solution)/shard_map/ppermute | solution.py:35
  351.9 2.3 copy-start.7
  351.9 2.3 copy-start.8
  351.9 2.3 copy-start.9
  351.9 2.3 copy-start.10
  351.9 2.3 copy-start.11
  352.0 2.3 copy-start.12
  352.0 2.3 copy-start.13
  352.0 2.3 copy-start.17
  381.7 4.6 %copy-start.15 = (s32[4]{0:T(128)S(1)}, s32[4]{0:T(128)}, u32[]{:S(2)}) copy-start(s32[4]{0:T(128)} %iota_multiply_fusion) | copy-start | bytes 52
  381.7 4.6 %copy-start.16 = (s32[64]{0:T(128)S(1)}, s32[64]{0:T(128)}, u32[]{:S(2)}) copy-start(s32[64]{0:T(128)} %iota_add_fusion) | copy-start | bytes 772
  381.8 10.3 %collective-permute-start.3 = (bf16[2,1,64,1024]{3,2,1,0:T(8,128)(2,1)S(1)}, bf16[2,1,64,1024]{3,2,1,0:T(8,128)(2,1)}, u32[]{:S(2)}, u32[]{:S(2)}) collective-permute-start(bf16[2,1,64,1024]{3,2,1,0:T(8,128)(2,1)S(1)} %get-tuple-element.20), channel_id=1, source_target_pairs={{0,4},{4,0},{8,12},{12,8},{1,5},{5,1},{9,13},{13,9},{2,6},{6,2},{1... | collective-permute-start | bytes 786440 | tf_op jit(solution)/shard_map/ppermute | solution.py:21
  382.2 21.7 %collective-permute-start.4 = (bf16[2,1,64,1024]{3,2,1,0:T(8,128)(2,1)S(1)}, bf16[2,1,64,1024]{3,2,1,0:T(8,128)(2,1)S(1)}, u32[]{:S(2)}, u32[]{:S(2)}) collective-permute-start(bf16[2,1,64,1024]{3,2,1,0:T(8,128)(2,1)S(1)} %get-tuple-element.21), channel_id=1, source_target_pairs={{0,8},{4,12},{8,0},{12,4},{1,9},{5,13},{9,1},{13,5},{2,10},{6,14},... | collective-permute-start | bytes 786440 | tf_op jit(solution)/shard_map/ppermute | solution.py:21
  385.5 22.3 %collective-permute-start.5 = (bf16[2,1,64,1024]{3,2,1,0:T(8,128)(2,1)S(1)}, bf16[2,1,64,1024]{3,2,1,0:T(8,128)(2,1)S(1)}, u32[]{:S(2)}, u32[]{:S(2)}) collective-permute-start(bf16[2,1,64,1024]{3,2,1,0:T(8,128)(2,1)S(1)} %get-tuple-element.18), channel_id=1, source_target_pairs={{0,12},{4,8},{8,4},{12,0},{1,13},{5,9},{9,5},{13,1},{2,14},{6,10},... | collective-permute-start | bytes 786440 | tf_op jit(solution)/shard_map/ppermute | solution.py:21
  416.0 15.3 %copy-start.14 = (f32[512]{0:T(512)S(1)}, f32[512]{0:T(512)}, u32[]{:S(2)}) copy-start(f32[512]{0:T(512)} %param.15) | copy-start | bytes 6148
  416.0 17.1 %copy-start.1 = (bf16[512,1024]{1,0:T(8,128)(2,1)S(1)}, bf16[512,1024]{1,0:T(8,128)(2,1)}, u32[]{:S(2)}) copy-start(bf16[512,1024]{1,0:T(8,128)(2,1)} %param.10) | copy-start | bytes 3145732
Sparse Core Ops, SparseCore 0:
  10.3 25.2 all-gather.2
  37.1 218.1 all-gather.4
